TPU v7x, 256 devices: a whole 4x4x8 slice. The times are simulated.
256 devices in a mesh: dp: 8 (over x, core), expert: 32 (over z, y).
Axes of the slice: x: 4, y: 4, z: 8, core: 2. Of those that a mesh axis runs over, the one named last changes fastest.
Arguments:
- out_grad: bfloat16 [32768, 2048], P(('dp', 'expert')), may hold values from -6 to 6
- combine: bfloat16 [32768, 6], P(('dp', 'expert')), may hold values from 0.049804688 to 0.59765625
- expert_ids: int32 [32768, 6], P(('dp', 'expert')), may hold values from 0 to 31, all different within a row; in each aligned block of 128 rows (0 to 127, 128 to 255, ...) at most 32 rows name the same one
- hidden: bfloat16 [32, 256, 32, 1408], P('expert', 'dp'), may hold values from -0.59765625 to 0.59765625
- w_down: bfloat16 [32, 2048, 1408], P('expert'), may hold values from -0.15625 to 0.15625
Outputs:
- grad_hidden: bfloat16 [32, 256, 32, 1408], P('expert', 'dp')
- grad_down: bfloat16 [32, 2048, 1408], P('expert', 'dp')
- grad_probs: float32 [32768, 6], P(('dp', 'expert'))
Inputs may be any that keep to these rules, and one draw needn't show every extreme that they name: `expert_ids`: each row names 6 different experts. Among the 128 rows of one source device no expert is named more than 32 times, and in every draw some expert is named exactly 32 times by the rows of some device.
All inputs are finite; a program needn't handle non-finite values.
Results may differ from a plain program's by a relative error of at most 0.013.
Values may be sent and summed in bfloat16 or wider, within the bound.
A program may use at most 64 MiB of HBM per device.

v0:
```python
import jax
import jax.numpy as jnp
from jax import lax
from jax.sharding import PartitionSpec as P


def body(out_grad, combine, expert_ids, hidden, w_down):
    tok_rows, picks = expert_ids.shape
    local_experts, senders, capacity, inner = hidden.shape
    model_width = out_grad.shape[1]
    experts_all = local_experts * lax.axis_size("expert")
    chosen = expert_ids.reshape(-1)
    onehot = (chosen[:, None] == jnp.arange(experts_all, dtype=jnp.int32)[None, :]).astype(
        jnp.int32
    )
    before = jnp.cumsum(onehot, axis=0) - onehot
    slot_rank = jnp.sum(before * onehot, axis=1)
    bucket_pos = chosen * capacity + slot_rank
    repeated = jnp.broadcast_to(out_grad[:, None, :], (tok_rows, picks, model_width)).reshape(
        -1, model_width
    )
    send_grad = (
        jnp.zeros((experts_all * capacity, model_width), out_grad.dtype)
        .at[bucket_pos]
        .set(repeated)
    )
    send_prob = (
        jnp.zeros((experts_all * capacity,), combine.dtype).at[bucket_pos].set(combine.reshape(-1))
    )
    recv_grad, recv_prob = (
        lax.all_to_all(
            send_grad.reshape(experts_all, 1, capacity, model_width),
            "expert",
            split_axis=0,
            concat_axis=1,
            tiled=True,
        ),
        lax.all_to_all(
            send_prob.reshape(experts_all, 1, capacity),
            "expert",
            split_axis=0,
            concat_axis=1,
            tiled=True,
        ),
    )
    hidden_grads, slot_grads, scaled_rows, saved_rows = ([], [], [], [])
    expert = 0
    grad_rows = recv_grad[expert].reshape(-1, model_width)
    slot_prob = recv_prob[expert].reshape(-1, 1).astype(jnp.float32)
    saved = hidden[expert].reshape(-1, inner)
    projected = jnp.dot(grad_rows, w_down[expert], preferred_element_type=jnp.float32)
    hidden_grads.append(
        (slot_prob * projected).astype(jnp.bfloat16).reshape(senders, capacity, inner)
    )
    slot_grads.append(jnp.sum(projected * saved, axis=1).reshape(senders, capacity))
    scaled_rows.append((slot_prob * grad_rows).astype(jnp.bfloat16))
    saved_rows.append(saved)
    expert = 0
    left = scaled_rows[expert]
    blocks = lax.dot_general(
        left, saved_rows[expert], (((0,), (0,)), ((), ())), preferred_element_type=jnp.float32
    )
    summed = lax.psum_scatter(
        blocks.astype(jnp.bfloat16), "dp", scatter_dimension=0, tiled=True
    ).astype(jnp.float32)
    grad_down = jnp.transpose(
        summed.reshape(summed.shape[0], local_experts, inner), (1, 0, 2)
    ).astype(jnp.bfloat16)
    returned = lax.all_to_all(
        jnp.stack(slot_grads), "expert", split_axis=1, concat_axis=0, tiled=True
    )
    grad_probs = returned.reshape(-1)[bucket_pos].reshape(tok_rows, picks)
    return (jnp.stack(hidden_grads), grad_down, grad_probs)


def solution(mesh):
    in_specs = (
        P(("dp", "expert"), None),
        P(("dp", "expert"), None),
        P(("dp", "expert"), None),
        P("expert", "dp", None, None),
        P("expert", None, None),
    )
    out_specs = (P("expert", "dp", None, None), P("expert", "dp", None), P(("dp", "expert"), None))
    return jax.shard_map(body, mesh=mesh, in_specs=in_specs, out_specs=out_specs, check_vma=False)
```

profile of v0, /device:TPU:8, one launch (start us, length us, event | category | flops | bytes accessed | tf_op | source)
XLA Modules:
  0.0 215.7 jit_solution(2342618734363493830)
XLA Ops:
  7.2 0.7 broadcast_multiply_fusion
  7.9 0.8 copy.15
  8.6 0.1 eq.29
  8.8 0.1 eq.25
  8.9 0.8 copy.18
  9.7 0.1 reshape.125
  9.9 0.1 copy.14
  10.0 0.1 mul.41
  10.2 1.7 reduce-window.6
  11.9 0.3 slice_reduce_fusion
  12.2 0.1 fusion.6
  12.3 8.6 %scatter_custom_fusion = bf16[1024]{0:T(1024)(128)(2,1)S(1)} fusion(s32[768]{0:T(1024)S(1)} %fusion.8, bf16[768]{0:T(1024)(128)(2,1)S(1)} %reshape.125, bf16[]{:T(256)} %constant.5.clone.1), kind=kCustom, calls=%fused_computation.24 | custom fusion | bytes 2050 | tf_op jit(solution)/shard_map/scatter | solution.py:28
  21.0 0.7 reshape.137
  21.6 11.7 %all-to-all-start = ((bf16[32,1,32]{2,1,0:T(2,128)(2,1)}), bf16[32,1,32]{2,1,0:T(2,128)(2,1)S(1)}, u32[]{:S(2)}, u32[]{:S(2)}) async-start(bf16[32,1,32]{2,1,0:T(2,128)(2,1)} %reshape.137), calls=%async_computation | async-start | bytes 32768 | tf_op jit(solution)/shard_map/all_to_all | solution.py:38
  33.4 3.6 %broadcast_in_dim.8 = bf16[128,6,2048]{2,1,0:T(8,128)(2,1)} broadcast(bf16[128,2048]{1,0:T(8,128)(2,1)} %param.5), dimensions={0,2} | broadcast | bytes 3670016 | tf_op jit(solution)/shard_map/broadcast_in_dim | solution.py:19
  37.0 4.9 %reshape.133 = bf16[768,2048]{1,0:T(8,128)(2,1)S(1)} reshape(bf16[128,6,2048]{2,1,0:T(8,128)(2,1)} %broadcast_in_dim.8) | data formatting | bytes 6291456 | tf_op jit(solution)/shard_map/reshape | solution.py:19
  41.9 9.4 %scatter_custom_fusion.1 = bf16[1024,2048]{1,0:T(8,128)(2,1)} fusion(s32[768]{0:T(1024)S(1)} %fusion.8, bf16[768,2048]{1,0:T(8,128)(2,1)S(1)} %reshape.133, bf16[]{:T(256)} %constant.5.clone.1), kind=kCustom, calls=%fused_computation.9 | custom fusion | bytes 4194306 | tf_op jit(solution)/shard_map/scatter | solution.py:25
  51.2 0.0 all-to-all-done
  51.2 10.0 %all-to-all-start.1 = ((bf16[32,1,32,2048]{3,2,1,0:T(8,128)(2,1)}), bf16[32,1,32,2048]{3,2,1,0:T(8,128)(2,1)}, u32[]{:S(2)}, u32[]{:S(2)}) async-start(bf16[32,1,32,2048]{3,2,1,0:T(8,128)(2,1)} %bitcast.39), calls=%async_computation.1 | async-start | bytes 8388608 | tf_op jit(solution)/shard_map/all_to_all | solution.py:31
  61.2 0.0 reduce-scatter.2.cloned.1.call-start
  61.3 92.9 %all-to-all-done.1 = bf16[32,1,32,2048]{3,2,1,0:T(8,128)(2,1)} async-done(((bf16[32,1,32,2048]{3,2,1,0:T(8,128)(2,1)}), bf16[32,1,32,2048]{3,2,1,0:T(8,128)(2,1)}, u32[]{:S(2)}, u32[]{:S(2)}) %all-to-all-start.1) | async-done | bytes 4194336 | tf_op jit(solution)/shard_map/all_to_all | solution.py:31
  154.2 0.0 copy-start
  154.2 3.1 %multiply_convert_fusion = bf16[32,1,32,2048]{3,2,1,0:T(8,128)(2,1)S(1)} fusion(bf16[32,1,32,2048]{3,2,1,0:T(8,128)(2,1)} %all-to-all-done.1, f32[32,32]{1,0:T(8,128)S(1)} %bitcast.41), kind=kLoop, calls=%fused_computation.3 | loop fusion | flops 6291456 | bytes 8392704 | tf_op jit(solution)/shard_map/convert_element_type | solution.py:56
  157.3 0.0 copy-done
  157.3 8.8 %convolution_convert_fusion = bf16[2048,1408]{1,0:T(8,128)(2,1)} fusion(bf16[1024,2048]{1,0:T(8,128)(2,1)S(1)} %bitcast.40, bf16[1024,1408]{1,0:T(8,128)(2,1)S(1)} %bitcast.43), kind=kOutput, calls=%fused_computation.4 | convolution fusion | flops 5908463616 | bytes 12845056 | tf_op jit(solution)/shard_map/dot_general | solution.py:60
  166.1 0.0 reduce-scatter.2.cloned.1.call-update
  166.1 0.1 convert_reduce_fusion
  166.1 0.1 reshape.111
  166.2 11.4 %multiply_reduce_fusion = (f32[1024]{0:T(1024)S(1)}, bf16[1024,1408]{1,0:T(8,128)(2,1)}) fusion(bf16[1,32,32,1408]{3,2,1,0:T(8,128)(2,1)S(1)} %copy-done, f32[1024]{0:T(1024)S(1)} %reshape.111, bf16[1024,2048]{1,0:T(8,128)(2,1)} %bitcast.2, bf16[1,2048,1408]{2,1,0:T(8,128)(2,1)} %param.9), kind=kOutput, calls=%fused_computation.7 | convolution fusion | flops 5912787968 | bytes 15736832 | tf_op jit(solution)/shard_map/dot_general | solution.py:51
  177.6 0.7 stack_reshape.7
  178.3 7.4 %all-to-all-start.2 = ((f32[1,32,32]{2,0,1:T(1,128)}), f32[1,32,32]{2,0,1:T(1,128)S(1)}, u32[]{:S(2)}, u32[]{:S(2)}) async-start(f32[1,32,32]{2,0,1:T(1,128)} %stack_reshape.7), calls=%async_computation.3 | async-start | bytes 32768 | tf_op jit(solution)/shard_map/all_to_all | solution.py:69
  185.7 8.5 %all-to-all-done.2 = f32[1,32,32]{2,0,1:T(1,128)S(1)} async-done(((f32[1,32,32]{2,0,1:T(1,128)}), f32[1,32,32]{2,0,1:T(1,128)S(1)}, u32[]{:S(2)}, u32[]{:S(2)}) %all-to-all-start.2) | async-done | bytes 4128 | tf_op jit(solution)/shard_map/all_to_all | solution.py:69
  194.2 0.5 broadcast.67
  194.8 0.7 reduce.11
  195.5 0.1 reshape.109
  195.5 3.2 %gather_fusion = f32[768]{0:T(1024)S(1)} fusion(f32[1024]{0:T(1024)S(1)} %reshape.109, s32[1024]{0:T(1024)S(1)} %pad_clamp_fusion), kind=kCustom, calls=%fused_computation | custom fusion | bytes 9216 | tf_op jit(solution)/shard_map/gather | solution.py:72
  198.7 0.1 reshape.110
  198.9 0.7 copy.20
  199.5 9.4 %reduce-scatter.2.cloned.1.call-done = bf16[256,1408]{1,0:T(8,128)(2,1)} async-done(((bf16[2048,1408]{1,0:T(8,128)(2,1)}), bf16[256,1408]{1,0:T(8,128)(2,1)}) %reduce-scatter.2.cloned.1.call-update) | async-done | bytes 720912 | tf_op jit(solution)/shard_map/reduce_scatter | solution.py:63
  (5 shorter events, 0.1 us)
Async XLA Ops:
  21.6 29.6 %all-to-all-start = ((bf16[32,1,32]{2,1,0:T(2,128)(2,1)}), bf16[32,1,32]{2,1,0:T(2,128)(2,1)S(1)}, u32[]{:S(2)}, u32[]{:S(2)}) async-start(bf16[32,1,32]{2,1,0:T(2,128)(2,1)} %reshape.137), calls=%async_computation | async-start | bytes 32768 | tf_op jit(solution)/shard_map/all_to_all | solution.py:38
  51.2 103.0 %all-to-all-start.1 = ((bf16[32,1,32,2048]{3,2,1,0:T(8,128)(2,1)}), bf16[32,1,32,2048]{3,2,1,0:T(8,128)(2,1)}, u32[]{:S(2)}, u32[]{:S(2)}) async-start(bf16[32,1,32,2048]{3,2,1,0:T(8,128)(2,1)} %bitcast.39), calls=%async_computation.1 | async-start | bytes 8388608 | tf_op jit(solution)/shard_map/all_to_all | solution.py:31
  61.2 147.6 %reduce-scatter.2.cloned.1.call-start = ((), (), s32[]{:S(2)}) async-start(), calls=%async_computation.4 | async-start | bytes 6488064 | tf_op jit(solution)/shard_map/reduce_scatter | solution.py:63
  154.2 3.1 %copy-start = (bf16[1,32,32,1408]{3,2,1,0:T(8,128)(2,1)S(1)}, bf16[1,32,32,1408]{3,2,1,0:T(8,128)(2,1)}, u32[]{:S(2)}) copy-start(bf16[1,32,32,1408]{3,2,1,0:T(8,128)(2,1)} %param.8) | copy-start | bytes 8650756
  178.3 16.0 %all-to-all-start.2 = ((f32[1,32,32]{2,0,1:T(1,128)}), f32[1,32,32]{2,0,1:T(1,128)S(1)}, u32[]{:S(2)}, u32[]{:S(2)}) async-start(f32[1,32,32]{2,0,1:T(1,128)} %stack_reshape.7), calls=%async_computation.3 | async-start | bytes 32768 | tf_op jit(solution)/shard_map/all_to_all | solution.py:69
Sparse Core Ops, SparseCore 0:
  166.2 42.6 reduce-scatter.1
where the time goes:
time: 216 us
  waiting for transfers between devices  111 us (51%)
  local copies, waits for them, and re-layouts  35 us (16%)
  starting transfers between devices  29.2 us (14%)
  matrix products  20.1 us (9%)
  between operations  14.2 us (7%)
  other arithmetic  6.45 us (3%)
    all_to_all x1, waiting for transfers between devices, body(): lax.all_to_all(send_grad.reshape(experts_all, 1, capacity, model_width),...  92.9 us
    all_to_all x1, starting transfers between devices, body(): lax.all_to_all(send_prob.reshape(experts_all, 1, capacity), 'expert', spl...  11.7 us
    dot_general x1, matrix products, body(): jnp.dot(grad_rows, w_down[expert], preferred_element_type=jnp.float32)  11.4 us
    all_to_all x1, starting transfers between devices, body(): lax.all_to_all(send_grad.reshape(experts_all, 1, capacity, model_width),...  10 us
    reduce_scatter x1, waiting for transfers between devices, body(): lax.psum_scatter(blocks.astype(jnp.bfloat16), 'dp', scatter_dimension=0,...  9.37 us
    scatter x1, local copies, waits for them, and re-layouts, body(): send_grad = jnp.zeros((experts_all * capacity, model_width), out_grad.dty...  9.35 us
    dot_general x1, matrix products, body(): lax.dot_general(left, saved_rows[expert], (((0,), (0,)), ((), ())), prefe...  8.77 us
    scatter x1, local copies, waits for them, and re-layouts, body(): jnp.zeros((experts_all * capacity,), combine.dtype).at[bucket_pos]  8.61 us
  transfers between devices with their start and end apart: 4, of which 3 were waited for; matrix products, arithmetic and copies ran while one was open for 16% of the time, Pallas kernels for 0%

commit v1 on v0

v1 whole, which is shorter than its diff:
```python
import functools

import jax
import jax.numpy as jnp
from jax import lax
from jax.experimental import pallas as pl
from jax.experimental.pallas import tpu as pltpu
from jax.sharding import PartitionSpec as P

MESH = pl.DeviceIdType.MESH
F32 = jnp.float32
BF16 = jnp.bfloat16
X, Y, Z = 4, 4, 8
PHASES = 2
RELAY_LAG = 2
ARRIVE_LAG = 4


def column_chunks(width):
    step = 512
    return [(at, min(step, width - at)) for at in range(0, width, step)]


def kernel(
    tok, ids, comb, hid_in, w_in, gh, gd, gp,
    own, zbuf, tab, pick, sel, relay, rows, prow, hid, phid, wv, acc, ghb,
    sums, send2, direct, relayed, relay_in, final_in, gdb, sg, sgy, sgu, sgz,
    sems,
):
    tokens, group_cols = own.shape[1:]
    sub = group_cols // X
    cap = tokens // Y
    inner = hid.shape[-1]
    chunks = column_chunks(inner)
    dp, ex = lax.axis_index("dp"), lax.axis_index("expert")
    x, core = dp // 2, dp % 2
    z, y = ex // Y, ex % Y
    y_a, y_b, y_far = y + 1 - 2 * (y % 2), Y - 1 - y, (y + 2) % Y

    def at_ex(zz, yy):
        return {"expert": zz * Y + yy}

    def at_dp(xx, cc):
        return {"dp": xx * 2 + cc}

    up, down = at_ex((z + 1) % Z, y), at_ex((z + Z - 1) % Z, y)
    side_a, side_b, side_far = at_ex(z, y_a), at_ex(z, y_b), at_ex(z, y_far)
    right, left = at_dp((x + 1) % X, core), at_dp((x + X - 1) % X, core)
    partner = at_dp(x, 1 - core)

    taken = [0]
    started = []

    def sem():
        taken[0] += 1
        return sems.at[taken[0] - 1]

    def local(src, dst):
        copy = pltpu.make_async_copy(src, dst, sem())
        copy.start()
        return copy

    def remote(src, dst, device):
        copy = pltpu.make_async_remote_copy(
            src_ref=src, dst_ref=dst, send_sem=sem(), recv_sem=sem(),
            device_id=device, device_id_type=MESH,
        )
        copy.start()
        started.append(copy)
        return copy

    own_loads = []
    for g in range(2 * PHASES):
        ph, cc = g // 2, g % 2
        own_loads.append([
            local(tok.at[:, pl.ds(q * 2 * 256 + cc * 256 + ph * sub, sub)],
                  own.at[g, :, pl.ds(q * sub, sub)])
            for q in range(X)
        ])
    hid_load = local(hid_in, hid)
    w_loads = []
    for ph in range(PHASES):
        for cc in range(2):
            for q in range(X):
                w_loads.append(local(
                    w_in.at[pl.ds(q * 512 + cc * 256 + ph * sub, sub)],
                    wv.at[ph, pl.ds(cc * group_cols + q * sub, sub)]))

    barrier = pltpu.get_barrier_semaphore()
    peers = [at_ex((z + d) % Z, y) for d in range(1, Z)]
    peers += [side_a, side_b, side_far, right, left, partner]
    for peer in peers:
        pl.semaphore_signal(barrier, inc=1, device_id=peer, device_id_type=MESH)

    ids_f = ids[...].astype(F32)
    comb_f = comb[...].astype(F32)
    picks = ids_f.shape[0]
    pad = 8 - picks
    tab[0] = jnp.concatenate([
        ids_f, jnp.full((pad, tokens), -1.0, F32), comb_f, jnp.zeros((pad, tokens), F32)
    ], axis=0).astype(BF16)
    before = (
        lax.broadcasted_iota(jnp.int32, (tokens, tokens), 0)
        < lax.broadcasted_iota(jnp.int32, (tokens, tokens), 1)
    ).astype(F32).astype(BF16)
    slot_of_row = lax.broadcasted_iota(jnp.int32, (cap, tokens), 0).astype(F32)

    def make_pick(si):
        table = tab[si].astype(F32)
        named, weight = table[0:8], table[8:16]
        chosen, probs = [], []
        for yy in (y_a, y_far, y_b, y):
            hit = named == (z * Y + yy).astype(F32)
            chosen.append(jnp.sum(jnp.where(hit, 1.0, 0.0), axis=0, keepdims=True))
            probs.append(jnp.sum(jnp.where(hit, weight, 0.0), axis=0, keepdims=True))
        marks = jnp.concatenate(chosen + [jnp.zeros((4, tokens), F32)], axis=0)
        rank = jnp.dot(marks.astype(BF16), before, preferred_element_type=F32)
        blocks = []
        for b in range(4):
            slot = jnp.where(chosen[b] > 0.5, rank[b:b + 1], -1.0)
            blocks.append(jnp.where(slot_of_row == slot, probs[b], 0.0))
        pick[si] = jnp.concatenate(blocks, axis=0).astype(BF16)

    make_pick(0)
    for load in own_loads[0] + own_loads[1]:
        load.wait()
    pl.semaphore_wait(barrier, len(peers))

    def source_z(si):
        return (z + (Z - si if si < 5 else si - 4)) % Z

    z_copies, tab_copies = {}, {}

    def token_block(direction, d, g):
        return own.at[g] if d == 0 else zbuf.at[direction, d - 1, g]

    def forward(direction, d, g):
        z_copies[direction, d + 1, g] = remote(
            token_block(direction, d, g), zbuf.at[direction, d, g], (up, down)[direction])

    def tab_index(direction, d):
        return 0 if d == 0 else d + 4 * direction

    def forward_tab(direction, d):
        tab_copies[direction, d + 1] = remote(
            tab.at[tab_index(direction, d)], tab.at[tab_index(direction, d + 1)],
            (up, down)[direction])

    y_copies, relay_copies, events = {}, {}, {}

    def unit(ph, ev, g, src, si):
        u = 2 * ev + len(events.setdefault(ev, []))
        zs = source_z(si)
        block = jnp.dot(pick[si], src[...], preferred_element_type=F32).astype(BF16)
        for b in range(3):
            sel[u, b] = block[b * cap:(b + 1) * cap]
        mine = pl.ds(pl.multiple_of(y * cap, cap), cap)
        rows[g, zs, mine] = block[3 * cap:]
        relay_copies[u] = remote(sel.at[u, 1], relay.at[u], side_a)
        y_copies.setdefault((ph, si), []).extend([
            remote(sel.at[u, 0], rows.at[g, zs, mine], side_a),
            remote(sel.at[u, 2], rows.at[g, zs, mine], side_b),
        ])
        events[ev].append((ph, u, g, si, zs))

    def pass_relays(ev):
        theirs = pl.ds(pl.multiple_of(y_a * cap, cap), cap)
        for ph, u, g, si, zs in events[ev]:
            relay_copies[u].wait_recv()
            y_copies[ph, si].append(remote(relay.at[u], rows.at[g, zs, theirs], side_b))

    prow_copies = {}

    def arrive(ph, sis):
        for si in sis:
            for copy in y_copies[ph, si]:
                copy.wait_recv()
            zs = source_z(si)
            prow_copies[ph, si] = remote(
                rows.at[2 * ph + 1 - core, zs], prow.at[ph, zs], partner)

    eye = (
        lax.broadcasted_iota(jnp.int32, (tokens, tokens), 0)
        == lax.broadcasted_iota(jnp.int32, (tokens, tokens), 1)
    )
    gh_copies = []
    w_waited = [False]

    def project(ph, sis):
        if not w_waited[0]:
            w_waited[0] = True
            hid_load.wait()
            for load in w_loads:
                load.wait()
        places = [source_z(si) for si in sis]
        halves = [
            jnp.concatenate([rows[2 * ph + cc, zs] for zs in places], axis=0) for cc in range(2)
        ]
        totals = [jnp.zeros((tokens, 1), F32) for _ in sis]
        for at, width in chunks:
            cols = pl.ds(at, width)
            value = jnp.dot(
                halves[0], wv[ph, 0:group_cols, cols], preferred_element_type=F32
            ) + jnp.dot(
                halves[1], wv[ph, group_cols:2 * group_cols, cols], preferred_element_type=F32)
            for n, zs in enumerate(places):
                part = value[n * tokens:(n + 1) * tokens]
                if ph > 0:
                    part = part + acc[zs, :, cols]
                if ph < PHASES - 1:
                    acc[zs, :, cols] = part
                else:
                    ghb[zs, :, cols] = part.astype(BF16)
                    totals[n] = totals[n] + jnp.sum(
                        part * hid[zs, :, cols].astype(F32), axis=1, keepdims=True)
        if ph == PHASES - 1:
            for n, zs in enumerate(places):
                gh_copies.append(local(ghb.at[zs], gh.at[zs]))
                sg[pl.ds(zs, 1), :] = jnp.sum(
                    jnp.where(eye, totals[n], 0.0), axis=0, keepdims=True)

    slices = [(x + 2) % X, (x + 1) % X, (x + X - 1) % X, x]
    half = sub // 2
    relay_sums, final_sums = {}, {}

    def weight_grad(ph, pair):
        lanes = [pl.ds(pl.multiple_of(q * sub, sub), sub) for q in slices[2 * pair:2 * pair + 2]]
        flat = Z * tokens
        mine = jnp.concatenate(
            [rows[2 * ph + core, :, :, q].reshape(flat, sub) for q in lanes], axis=1)
        others = jnp.concatenate(
            [prow[ph, :, :, q].reshape(flat, sub) for q in lanes], axis=1)
        contract = (((0,), (0,)), ((), ()))
        for at, width in chunks:
            cols = pl.ds(at, width)
            value = lax.dot_general(
                mine, hid[:, :, cols].reshape(flat, width), contract, preferred_element_type=F32
            ) + lax.dot_general(
                others, phid[:, :, cols].reshape(flat, width), contract,
                preferred_element_type=F32)
            first, second = value[0:sub], value[sub:2 * sub]
            if pair == 0:
                send2[ph, :, cols] = first.astype(BF16)
                direct[ph, 0, :, cols] = second[half:].astype(BF16)
                sums[ph, 0, :, cols] = second[0:half]
            else:
                direct[ph, 1, :, cols] = first[0:half].astype(BF16)
                sums[ph, 1, :, cols] = first[half:]
                sums[ph, 2, :, cols] = second[0:half]
                sums[ph, 3, :, cols] = second[half:]
        if pair == 0:
            relay_sums[ph] = [
                remote(send2.at[ph, pl.ds(0, half)], relay_in.at[ph, 0], right),
                remote(send2.at[ph, pl.ds(half, half)], relay_in.at[ph, 1], left),
            ]
            final_sums[ph] = [remote(direct.at[ph, 0], final_in.at[ph, 0, 1], right)]
        else:
            final_sums[ph].append(remote(direct.at[ph, 1], final_in.at[ph, 1, 0], left))

    def wait_partner(ph):
        if ph == 0:
            phid_copy.wait_recv()
        for si in range(Z):
            prow_copies[ph, si].wait_recv()

    def pass_sums(ph):
        for side in range(2):
            relay_sums[ph][side].wait_recv()
            relayed[ph, side] = (sums[ph, side] + relay_in[ph, side].astype(F32)).astype(BF16)
            final_sums[ph].append(
                remote(relayed.at[ph, side], final_in.at[ph, side, side], (right, left)[side]))

    gd_copies = []

    def finish_sums(ph):
        for copy in final_sums[ph]:
            copy.wait_recv()
        for part in range(2):
            gdb[ph, pl.ds(part * half, half)] = (
                sums[ph, 2 + part] + final_in[ph, 0, part].astype(F32)
                + final_in[ph, 1, part].astype(F32)
            ).astype(BF16)
        gd_copies.append(local(gdb.at[ph], gd.at[pl.ds(ph * sub, sub)]))

    for direction in range(2):
        forward_tab(direction, 0)
    for g in range(2):
        for direction in range(2):
            forward(direction, 0, g)
    phid_copy = remote(hid_in, phid, partner)

    arrivals = []
    for ph in range(PHASES):
        arrivals += [(8 * ph, ph, (0,))]
        arrivals += [(8 * ph + 2 * d, ph, (d, 4 + d)) for d in (1, 2, 3)]
        arrivals += [(8 * ph + 7, ph, (4,))]
    todo = {}
    for ev, ph, sis in arrivals:
        todo.setdefault(ev + ARRIVE_LAG, []).append((ph, sis))
    last = 8 * PHASES - 1

    for ev in range(8 * PHASES):
        ph, i = ev // 8, ev % 8
        g0 = 2 * ph
        if i == 0:
            unit(ph, ev, g0, own.at[g0], 0)
            unit(ph, ev, g0 + 1, own.at[g0 + 1], 0)
        elif i < 7:
            d, cc = (i + 1) // 2, (i + 1) % 2
            g = g0 + cc
            if ph == 0 and cc == 0:
                for direction in range(2):
                    tab_copies[direction, d].wait_recv()
                    if d < 4 - direction:
                        forward_tab(direction, d)
            for direction in range(2):
                z_copies[direction, d, g].wait_recv()
                if d < 3 or cc == direction:
                    forward(direction, d, g)
            if i in (5, 6) and ph + 1 < PHASES:
                for load in own_loads[g + 2]:
                    load.wait()
                for direction in range(2):
                    forward(direction, 0, g + 2)
            for direction in range(2):
                si = tab_index(direction, d)
                if ph == 0 and cc == 0:
                    make_pick(si)
                unit(ph, ev, g, zbuf.at[direction, d - 1, g], si)
        else:
            if ph == 0:
                tab_copies[0, 4].wait_recv()
                make_pick(4)
            for direction in range(2):
                z_copies[direction, 4, g0 + direction].wait_recv()
                unit(ph, ev, g0 + direction, zbuf.at[direction, 3, g0 + direction], 4)
        if ev >= RELAY_LAG:
            pass_relays(ev - RELAY_LAG)
        for ready_ph, sis in todo.pop(ev, []):
            arrive(ready_ph, sis)
            project(ready_ph, sis)
        if ph > 0 and i == 4:
            wait_partner(ph - 1)
            weight_grad(ph - 1, 0)
        if ph > 0 and i == 5:
            weight_grad(ph - 1, 1)
        if ph > 0 and i == 7:
            pass_sums(ph - 1)

    for ev in range(last - RELAY_LAG + 1, last + 1):
        pass_relays(ev)
    rest = [item for ev in sorted(todo) for item in todo[ev]]
    for ready_ph, sis in rest:
        arrive(ready_ph, sis)
    for ready_ph, sis in rest[:-1]:
        project(ready_ph, sis)
    wait_partner(PHASES - 1)
    weight_grad(PHASES - 1, 0)
    weight_grad(PHASES - 1, 1)
    project(*rest[-1])

    sgy[y] = sg[...]
    back = [remote(sg, sgy.at[y], peer) for peer in (side_a, side_b, side_far)]
    finish_sums(0)
    pass_sums(PHASES - 1)
    for copy in back:
        copy.wait_recv()
    for zz in range(Z):
        for yy in range(Y):
            sgu[zz, yy:yy + 1] = sgy[yy, zz:zz + 1]
        sgu[zz, Y:8] = jnp.zeros((8 - Y, tokens), F32)
    sgz[z] = sgu[z]
    back = [remote(sgu.at[(z + d) % Z], sgz.at[z], at_ex((z + d) % Z, y)) for d in range(1, Z)]

    row_id = lax.broadcasted_iota(jnp.int32, (8 * Z, tokens), 0)
    expert_of_row = jnp.where(row_id % 8 < Y, row_id // 8 * Y + row_id % 8, -1).astype(F32)
    marks = jnp.zeros((8 * Z, tokens), F32)
    for k in range(picks):
        marks = marks + jnp.where(expert_of_row == ids_f[k:k + 1], 1.0, 0.0)
    rank = jnp.dot(marks.astype(BF16), before, preferred_element_type=F32)
    slot = jnp.where(marks > 0.5, rank, -1.0)
    for copy in back:
        copy.wait_recv()
    table = sgz[...].reshape(8 * Z, tokens)
    values = jnp.zeros((8 * Z, cap), F32)
    for yy in range(Y):
        values = jnp.where(y == yy, table[:, yy * cap:(yy + 1) * cap], values)
    found = jnp.zeros((8 * Z, tokens), F32)
    for cc in range(cap):
        found = jnp.where(slot == float(cc), values[:, cc:cc + 1], found)
    for k in range(picks):
        gp[k:k + 1, :] = jnp.sum(
            jnp.where(expert_of_row == ids_f[k:k + 1], found, 0.0), axis=0, keepdims=True
        ) / comb_f[k:k + 1]

    finish_sums(PHASES - 1)
    for copy in started:
        copy.wait_send()
    for copy in gh_copies + gd_copies:
        copy.wait()


def body(out_grad, combine, expert_ids, hidden, w_down):
    tokens, picks = expert_ids.shape
    width = out_grad.shape[1]
    cap, inner = hidden.shape[2], hidden.shape[3]
    groups = 2 * PHASES
    gcols = width // groups
    sub = gcols // X
    flat = (Z, Y * cap)
    vmem = lambda shape, kind=BF16: pltpu.VMEM(shape, kind)
    anywhere = pl.BlockSpec(memory_space=pl.ANY)
    in_vmem = pl.BlockSpec(memory_space=pltpu.VMEM)
    grad_hidden, grad_down, grad_probs = pl.pallas_call(
        kernel,
        out_shape=(
            jax.ShapeDtypeStruct(flat + (inner,), BF16),
            jax.ShapeDtypeStruct((PHASES * sub, inner), BF16),
            jax.ShapeDtypeStruct((picks, tokens), F32),
        ),
        in_specs=[anywhere, in_vmem, in_vmem, anywhere, anywhere],
        out_specs=(anywhere, anywhere, in_vmem),
        scratch_shapes=[
            vmem((groups, tokens, gcols)),
            vmem((2, 4, groups, tokens, gcols)),
            vmem((Z, 16, tokens)),
            vmem((Z, tokens, tokens)),
            vmem((16 * PHASES, 3, cap, gcols)),
            vmem((16 * PHASES, cap, gcols)),
            vmem((groups,) + flat + (gcols,)),
            vmem((PHASES,) + flat + (gcols,)),
            vmem(flat + (inner,)),
            vmem(flat + (inner,)),
            vmem((PHASES, 2 * gcols, inner)),
            vmem(flat + (inner,), F32),
            vmem(flat + (inner,)),
            vmem((PHASES, 4, sub // 2, inner), F32),
            vmem((PHASES, sub, inner)),
            vmem((PHASES, 2, sub // 2, inner)),
            vmem((PHASES, 2, sub // 2, inner)),
            vmem((PHASES, 2, sub // 2, inner)),
            vmem((PHASES, 2, 2, sub // 2, inner)),
            vmem((PHASES, sub, inner)),
            vmem((Z, tokens), F32),
            vmem((Y, Z, tokens), F32),
            vmem((Z, 8, tokens), F32),
            vmem((Z, 8, tokens), F32),
            pltpu.SemaphoreType.DMA((512,)),
        ],
        compiler_params=pltpu.CompilerParams(
            collective_id=0, has_side_effects=True, vmem_limit_bytes=60 * 2**20),
    )(
        out_grad, expert_ids.T, combine.T,
        hidden.reshape(flat + (inner,)), w_down[0],
    )
    return (
        grad_hidden.reshape(hidden.shape),
        grad_down[None],
        grad_probs.T,
    )


def solution(mesh):
    in_specs = (
        P(("dp", "expert"), None),
        P(("dp", "expert"), None),
        P(("dp", "expert"), None),
        P("expert", "dp", None, None),
        P("expert", None, None),
    )
    out_specs = (P("expert", "dp", None, None), P("expert", "dp", None), P(("dp", "expert"), None))
    return jax.shard_map(body, mesh=mesh, in_specs=in_specs, out_specs=out_specs, check_vma=False)
```

time: 216 us -> 92.6 us (0.43)
  waiting for transfers between devices: 111 us -> 0 us
  Pallas kernels: 0 us -> 85.8 us
  local copies, waits for them, and re-layouts: 35 us -> 5.13 us
  starting transfers between devices: 29.2 us -> 0 us
  matrix products: 20.1 us -> 0 us
  between operations: 14.2 us -> 0.66 us
  other arithmetic: 6.45 us -> 0 us
    all_to_all x3 -> x0, waiting for transfers between devices: 101 us -> none  [the longest x1 92.9 us: body(): lax.all_to_all(send_grad.reshape(experts_all, 1, capacity, model_width),...]
    pallas_call x0 -> x1, Pallas kernels: none -> 85.8 us  [body(): pl.pallas_call(kernel, out_shape=(jax.ShapeDtypeStruct(flat + (inner,), B...]
    all_to_all x3 -> x0, starting transfers between devices: 29.1 us -> none  [the longest x1 11.7 us: body(): lax.all_to_all(send_prob.reshape(experts_all, 1, capacity), 'expert', spl...]
    dot_general x2 -> x0, matrix products: 20.1 us -> none  [the longest x1 11.4 us: body(): jnp.dot(grad_rows, w_down[expert], preferred_element_type=jnp.float32)]
    scatter x2 -> x0, local copies, waits for them, and re-layouts: 18 us -> none  [the longest x1 9.35 us: body(): send_grad = jnp.zeros((experts_all * capacity, model_width), out_grad.dty...]
    reduce_scatter x1 -> x0, waiting for transfers between devices: 9.37 us -> none  [body(): lax.psum_scatter(blocks.astype(jnp.bfloat16), 'dp', scatter_dimension=0,...]
    reshape x5 -> x0, local copies, waits for them, and re-layouts: 5.9 us -> none  [the longest x1 4.87 us: body(): jnp.broadcast_to(out_grad[:, None, :], (tok_rows, picks, model_width))]
    broadcast_in_dim x1 -> x0, local copies, waits for them, and re-layouts: 3.64 us -> none  [body(): jnp.broadcast_to(out_grad[:, None, :], (tok_rows, picks, model_width))]
  transfers between devices with their start and end apart: 4 -> 0, of which waited for: 3 -> 0; matrix products, arithmetic and copies ran while one was open for 16% -> 0% of each run, Pallas kernels for 0% -> 0%
where the time goes in v1:
time: 92.6 us; the launch traced here: 91.6 us
  Pallas kernels  85.8 us (93%)
  local copies, waits for them, and re-layouts  5.13 us (6%)
    pallas_call x1, Pallas kernels, body(): pl.pallas_call(kernel, out_shape=(jax.ShapeDtypeStruct(flat + (inner,), B...  85.8 us
    unnamed x7, local copies, waits for them, and re-layouts  5.13 us

profile of v1, /device:TPU:8, one launch (start us, length us, event | category | flops | bytes accessed | tf_op | source)
XLA Modules:
  0.0 91.6 jit_solution(2072901181808679530)
XLA Ops:
  0.6 85.8 %shard_map.76 = (bf16[8,128,1408]{2,1,0:T(8,128)(2,1)}, bf16[256,1408]{1,0:T(8,128)(2,1)}, f32[6,128]{1,0:T(8,128)}) custom-call(bf16[128,2048]{1,0:T(8,128)(2,1)} %tok.1, s32[6,128]{1,0:T(8,128)} %bitcast.11, bf16[6,128]{1,0:T(8,128)(2,1)} %bitcast.13, bf16[8,128,1408]{2,1,0:T(8,128)(2,1)} %bitcast.9, bf16[2048,1408]{1,0:T(8,128)(2,1)} %bitcast.7), custom_call_target="tpu_custom_call" | custom-call | tf_op jit(solution)/shard_map/pallas_call | solution.py:414
  86.5 0.0 copy-start
  86.5 0.0 copy-start.1
  86.5 3.7 %copy.11 = bf16[1,32,32,1408]{3,2,1,0:T(8,128)(2,1)} copy(bf16[1,32,32,1408]{3,2,1,0:T(8,128)(2,1)} %bitcast.8) | data formatting | bytes 5767168
  90.2 0.0 copy-done
  90.2 0.9 copy.12
  91.0 0.0 copy-done.1
  91.0 0.6 copy.13
Async XLA Ops:
  86.5 3.7 %copy-start = (bf16[256,1408]{1,0:T(8,128)(2,1)S(1)}, bf16[256,1408]{1,0:T(8,128)(2,1)}, u32[]{:S(2)}) copy-start(bf16[256,1408]{1,0:T(8,128)(2,1)} %get-tuple-element.7) | copy-start | bytes 2162692
  86.5 4.5 %copy-start.1 = (f32[6,128]{1,0:T(8,128)S(1)}, f32[6,128]{1,0:T(8,128)}, u32[]{:S(2)}) copy-start(f32[6,128]{1,0:T(8,128)} %get-tuple-element.8) | copy-start | bytes 9220

commit v2 on v1

--- a/solution.py
+++ b/solution.py
@@ -12,8 +12,7 @@
 BF16 = jnp.bfloat16
 X, Y, Z = 4, 4, 8
 PHASES = 2
-RELAY_LAG = 2
-ARRIVE_LAG = 4
+ARRIVE_LAG = 2
 
 
 def column_chunks(width):
@@ -23,7 +22,7 @@
 
 def kernel(
     tok, ids, comb, hid_in, w_in, gh, gd, gp,
-    own, zbuf, tab, pick, sel, relay, rows, prow, hid, phid, wv, acc, ghb,
+    own, zbuf, tab, pick, sel, rows, prow, hid, phid, wv, acc, ghb,
     sums, send2, direct, relayed, relay_in, final_in, gdb, sg, sgy, sgu, sgz,
     sems,
 ):
@@ -87,8 +86,7 @@
                     wv.at[ph, pl.ds(cc * group_cols + q * sub, sub)]))
 
     barrier = pltpu.get_barrier_semaphore()
-    peers = [at_ex((z + d) % Z, y) for d in range(1, Z)]
-    peers += [side_a, side_b, side_far, right, left, partner]
+    peers = [up, down, side_a, side_b, side_far, right, left, partner]
     for peer in peers:
         pl.semaphore_signal(barrier, inc=1, device_id=peer, device_id_type=MESH)
 
@@ -146,7 +144,7 @@
             tab.at[tab_index(direction, d)], tab.at[tab_index(direction, d + 1)],
             (up, down)[direction])
 
-    y_copies, relay_copies, events = {}, {}, {}
+    y_copies, events = {}, {}
 
     def unit(ph, ev, g, src, si):
         u = 2 * ev + len(events.setdefault(ev, []))
@@ -156,18 +154,11 @@
             sel[u, b] = block[b * cap:(b + 1) * cap]
         mine = pl.ds(pl.multiple_of(y * cap, cap), cap)
         rows[g, zs, mine] = block[3 * cap:]
-        relay_copies[u] = remote(sel.at[u, 1], relay.at[u], side_a)
         y_copies.setdefault((ph, si), []).extend([
-            remote(sel.at[u, 0], rows.at[g, zs, mine], side_a),
-            remote(sel.at[u, 2], rows.at[g, zs, mine], side_b),
+            remote(sel.at[u, b], rows.at[g, zs, mine], peer)
+            for b, peer in ((1, side_far), (0, side_a), (2, side_b))
         ])
-        events[ev].append((ph, u, g, si, zs))
-
-    def pass_relays(ev):
-        theirs = pl.ds(pl.multiple_of(y_a * cap, cap), cap)
-        for ph, u, g, si, zs in events[ev]:
-            relay_copies[u].wait_recv()
-            y_copies[ph, si].append(remote(relay.at[u], rows.at[g, zs, theirs], side_b))
+        events[ev].append(u)
 
     prow_copies = {}
 
@@ -297,7 +288,6 @@
     todo = {}
     for ev, ph, sis in arrivals:
         todo.setdefault(ev + ARRIVE_LAG, []).append((ph, sis))
-    last = 8 * PHASES - 1
 
     for ev in range(8 * PHASES):
         ph, i = ev // 8, ev % 8
@@ -334,8 +324,6 @@
             for direction in range(2):
                 z_copies[direction, 4, g0 + direction].wait_recv()
                 unit(ph, ev, g0 + direction, zbuf.at[direction, 3, g0 + direction], 4)
-        if ev >= RELAY_LAG:
-            pass_relays(ev - RELAY_LAG)
         for ready_ph, sis in todo.pop(ev, []):
             arrive(ready_ph, sis)
             project(ready_ph, sis)
@@ -347,8 +335,6 @@
         if ph > 0 and i == 7:
             pass_sums(ph - 1)
 
-    for ev in range(last - RELAY_LAG + 1, last + 1):
-        pass_relays(ev)
     rest = [item for ev in sorted(todo) for item in todo[ev]]
     for ready_ph, sis in rest:
         arrive(ready_ph, sis)
@@ -409,7 +395,9 @@
     sub = gcols // X
     flat = (Z, Y * cap)
     vmem = lambda shape, kind=BF16: pltpu.VMEM(shape, kind)
+    in_place = lambda a: pltpu.with_memory_space_constraint(a, pltpu.HBM)
     anywhere = pl.BlockSpec(memory_space=pl.ANY)
+    in_hbm = pl.BlockSpec(memory_space=pltpu.HBM)
     in_vmem = pl.BlockSpec(memory_space=pltpu.VMEM)
     grad_hidden, grad_down, grad_probs = pl.pallas_call(
         kernel,
@@ -418,7 +406,7 @@
             jax.ShapeDtypeStruct((PHASES * sub, inner), BF16),
             jax.ShapeDtypeStruct((picks, tokens), F32),
         ),
-        in_specs=[anywhere, in_vmem, in_vmem, anywhere, anywhere],
+        in_specs=[in_hbm, in_vmem, in_vmem, in_hbm, in_hbm],
         out_specs=(anywhere, anywhere, in_vmem),
         scratch_shapes=[
             vmem((groups, tokens, gcols)),
@@ -426,7 +414,6 @@
             vmem((Z, 16, tokens)),
             vmem((Z, tokens, tokens)),
             vmem((16 * PHASES, 3, cap, gcols)),
-            vmem((16 * PHASES, cap, gcols)),
             vmem((groups,) + flat + (gcols,)),
             vmem((PHASES,) + flat + (gcols,)),
             vmem(flat + (inner,)),
@@ -448,10 +435,10 @@
             pltpu.SemaphoreType.DMA((512,)),
         ],
         compiler_params=pltpu.CompilerParams(
-            collective_id=0, has_side_effects=True, vmem_limit_bytes=60 * 2**20),
+            collective_id=0, has_side_effects=True, vmem_limit_bytes=46 * 2**20),
     )(
-        out_grad, expert_ids.T, combine.T,
-        hidden.reshape(flat + (inner,)), w_down[0],
+        in_place(out_grad), expert_ids.T, combine.T,
+        in_place(hidden.reshape(flat + (inner,))), in_place(w_down[0]),
     )
     return (
         grad_hidden.reshape(hidden.shape),

time: 92.6 us -> 88 us (0.950)
  Pallas kernels: 85.8 us -> 81.7 us
    pallas_call x1, Pallas kernels: 85.8 us -> 81.7 us  [body(): pl.pallas_call(kernel, out_shape=(jax.ShapeDtypeStruct(flat + (inner,), B...]
where the time goes in v2:
time: 88 us; the launch traced here: 86.8 us
  Pallas kernels  81.7 us (93%)
  local copies, waits for them, and re-layouts  4.39 us (5%)
    pallas_call x1, Pallas kernels, body(): pl.pallas_call(kernel, out_shape=(jax.ShapeDtypeStruct(flat + (inner,), B...  81.7 us
    unnamed x7, local copies, waits for them, and re-layouts  4.39 us

profile of v2, /device:TPU:8, one launch (start us, length us, event | category | flops | bytes accessed | tf_op | source)
XLA Modules:
  0.0 86.8 jit_solution(10749462579930507299)
XLA Ops:
  0.6 0.0 copy-start
  0.6 0.7 copy-done
  1.3 0.0 copy-start.1
  1.3 0.7 copy-done.1
  2.0 81.7 %shard_map.76 = (bf16[8,128,1408]{2,1,0:T(8,128)(2,1)S(1)}, bf16[256,1408]{1,0:T(8,128)(2,1)S(1)}, f32[6,128]{1,0:T(8,128)S(1)}) custom-call(bf16[128,2048]{1,0:T(8,128)(2,1)} %tok.1, s32[6,128]{1,0:T(8,128)S(1)} %bitcast.9, bf16[6,128]{1,0:T(8,128)(2,1)S(1)} %bitcast.11, bf16[8,128,1408]{2,1,0:T(8,128)(2,1)} %bitcast.13, bf16[2048,1408]{1,0:T(8,128)(2,1)} %bitcast.12), custom_call_target="tpu_custom_call" | custom-call | tf_op jit(solution)/shard_map/pallas_call | solution.py:402
  83.8 1.6 %copy.11 = bf16[1,32,32,1408]{3,2,1,0:T(8,128)(2,1)} copy(bf16[1,32,32,1408]{3,2,1,0:T(8,128)(2,1)S(1)} %bitcast.7) | data formatting | bytes 5767168
  85.3 0.9 copy.12
  86.2 0.6 copy.13
Async XLA Ops:
  0.6 0.7 copy-start
  1.3 0.7 copy-start.1

commit v3 on v2

--- a/solution.py
+++ b/solution.py
@@ -12,7 +12,7 @@
 BF16 = jnp.bfloat16
 X, Y, Z = 4, 4, 8
 PHASES = 2
-ARRIVE_LAG = 2
+ARRIVE_LAG = 4
 
 
 def column_chunks(width):
@@ -21,8 +21,8 @@
 
 
 def kernel(
-    tok, ids, comb, hid_in, w_in, gh, gd, gp,
-    own, zbuf, tab, pick, sel, rows, prow, hid, phid, wv, acc, ghb,
+    tok, ids_in, comb_in, hid_in, w_in, gh, gd, gp,
+    ids, comb, own, zbuf, tab, pick, sel, rows, prow, hid, phid, wv, acc, ghb,
     sums, send2, direct, relayed, relay_in, final_in, gdb, sg, sgy, sgu, sgz,
     sems,
 ):
@@ -68,6 +68,7 @@
         started.append(copy)
         return copy
 
+    table_loads = [local(ids_in, ids), local(comb_in, comb)]
     own_loads = []
     for g in range(2 * PHASES):
         ph, cc = g // 2, g % 2
@@ -90,6 +91,8 @@
     for peer in peers:
         pl.semaphore_signal(barrier, inc=1, device_id=peer, device_id_type=MESH)
 
+    for load in table_loads:
+        load.wait()
     ids_f = ids[...].astype(F32)
     comb_f = comb[...].astype(F32)
     picks = ids_f.shape[0]
@@ -280,6 +283,10 @@
             forward(direction, 0, g)
     phid_copy = remote(hid_in, phid, partner)
 
+    def own_units(ph):
+        for g in (2 * ph, 2 * ph + 1):
+            unit(ph, 8 * ph, g, own.at[g], 0)
+
     arrivals = []
     for ph in range(PHASES):
         arrivals += [(8 * ph, ph, (0,))]
@@ -293,8 +300,11 @@
         ph, i = ev // 8, ev % 8
         g0 = 2 * ph
         if i == 0:
-            unit(ph, ev, g0, own.at[g0], 0)
-            unit(ph, ev, g0 + 1, own.at[g0 + 1], 0)
+            if ph == 0:
+                own_units(0)
+                for load in own_loads[2] + own_loads[3]:
+                    load.wait()
+                own_units(1)
         elif i < 7:
             d, cc = (i + 1) // 2, (i + 1) % 2
             g = g0 + cc
@@ -308,8 +318,6 @@
                 if d < 3 or cc == direction:
                     forward(direction, d, g)
             if i in (5, 6) and ph + 1 < PHASES:
-                for load in own_loads[g + 2]:
-                    load.wait()
                 for direction in range(2):
                     forward(direction, 0, g + 2)
             for direction in range(2):
@@ -406,9 +414,11 @@
             jax.ShapeDtypeStruct((PHASES * sub, inner), BF16),
             jax.ShapeDtypeStruct((picks, tokens), F32),
         ),
-        in_specs=[in_hbm, in_vmem, in_vmem, in_hbm, in_hbm],
+        in_specs=[in_hbm] * 5,
         out_specs=(anywhere, anywhere, in_vmem),
         scratch_shapes=[
+            vmem((picks, tokens), jnp.int32),
+            vmem((picks, tokens)),
             vmem((groups, tokens, gcols)),
             vmem((2, 4, groups, tokens, gcols)),
             vmem((Z, 16, tokens)),
@@ -437,7 +447,7 @@
         compiler_params=pltpu.CompilerParams(
             collective_id=0, has_side_effects=True, vmem_limit_bytes=46 * 2**20),
     )(
-        in_place(out_grad), expert_ids.T, combine.T,
+        in_place(out_grad), in_place(expert_ids.T), in_place(combine.T),
         in_place(hidden.reshape(flat + (inner,))), in_place(w_down[0]),
     )
     return (

time: 88 us -> 82.8 us (0.941); the launches traced: 86.8 us -> 82.7 us
  Pallas kernels: 81.7 us -> 79 us
  local copies, waits for them, and re-layouts: 4.39 us -> 3.03 us
    pallas_call x1, Pallas kernels: 81.7 us -> 79 us  [body(): pl.pallas_call(kernel, out_shape=(jax.ShapeDtypeStruct(flat + (inner,), B...]
    unnamed x7 -> x3, local copies, waits for them, and re-layouts: 4.39 us -> 3.03 us
where the time goes in v3:
time: 82.8 us; the launch traced here: 82.7 us
  Pallas kernels  79 us (95%)
  local copies, waits for them, and re-layouts  3.03 us (4%)
    pallas_call x1, Pallas kernels, body(): pl.pallas_call(kernel, out_shape=(jax.ShapeDtypeStruct(flat + (inner,), B...  79 us
    unnamed x3, local copies, waits for them, and re-layouts  3.03 us

profile of v3, /device:TPU:8, one launch (start us, length us, event | category | flops | bytes accessed | tf_op | source)
XLA Modules:
  0.0 82.7 jit_solution(18143776257011919690)
XLA Ops:
  0.6 79.0 %shard_map.76 = (bf16[8,128,1408]{2,1,0:T(8,128)(2,1)S(1)}, bf16[256,1408]{1,0:T(8,128)(2,1)S(1)}, f32[6,128]{1,0:T(8,128)S(1)}) custom-call(bf16[128,2048]{1,0:T(8,128)(2,1)} %tok.1, s32[6,128]{1,0:T(8,128)} %bitcast.12, bf16[6,128]{1,0:T(8,128)(2,1)} %bitcast.13, bf16[8,128,1408]{2,1,0:T(8,128)(2,1)} %bitcast.11, bf16[2048,1408]{1,0:T(8,128)(2,1)} %bitcast.10), custom_call_target="tpu_custom_call" | custom-call | tf_op jit(solution)/shard_map/pallas_call | solution.py:410
  79.7 1.6 %copy.11 = bf16[1,32,32,1408]{3,2,1,0:T(8,128)(2,1)} copy(bf16[1,32,32,1408]{3,2,1,0:T(8,128)(2,1)S(1)} %bitcast.7) | data formatting | bytes 5767168
  81.3 0.9 %copy.12 = bf16[1,256,1408]{2,1,0:T(8,128)(2,1)} copy(bf16[1,256,1408]{2,1,0:T(8,128)(2,1)S(1)} %bitcast.8) | data formatting | bytes 1441792
  82.1 0.6 copy.13

commit v4 on v3

--- a/solution.py
+++ b/solution.py
@@ -281,7 +281,6 @@
     for g in range(2):
         for direction in range(2):
             forward(direction, 0, g)
-    phid_copy = remote(hid_in, phid, partner)
 
     def own_units(ph):
         for g in (2 * ph, 2 * ph + 1):
@@ -298,6 +297,8 @@
 
     for ev in range(8 * PHASES):
         ph, i = ev // 8, ev % 8
+        if ev == 5:
+            phid_copy = remote(hid_in, phid, partner)
         g0 = 2 * ph
         if i == 0:
             if ph == 0:
@@ -356,7 +357,6 @@
     sgy[y] = sg[...]
     back = [remote(sg, sgy.at[y], peer) for peer in (side_a, side_b, side_far)]
     finish_sums(0)
-    pass_sums(PHASES - 1)
     for copy in back:
         copy.wait_recv()
     for zz in range(Z):
@@ -365,6 +365,7 @@
         sgu[zz, Y:8] = jnp.zeros((8 - Y, tokens), F32)
     sgz[z] = sgu[z]
     back = [remote(sgu.at[(z + d) % Z], sgz.at[z], at_ex((z + d) % Z, y)) for d in range(1, Z)]
+    pass_sums(PHASES - 1)
 
     row_id = lax.broadcasted_iota(jnp.int32, (8 * Z, tokens), 0)
     expert_of_row = jnp.where(row_id % 8 < Y, row_id // 8 * Y + row_id % 8, -1).astype(F32)

time: 82.8 us -> 82.8 us (level)
  no operation moved by 1% of the time
where the time goes in v4:
time: 82.8 us; the launch traced here: 82.7 us
  Pallas kernels  79 us (95%)
  local copies, waits for them, and re-layouts  3.03 us (4%)
    pallas_call x1, Pallas kernels, body(): pl.pallas_call(kernel, out_shape=(jax.ShapeDtypeStruct(flat + (inner,), B...  79 us
    unnamed x3, local copies, waits for them, and re-layouts  3.03 us

profile of v4, /device:TPU:8, one launch (start us, length us, event | category | flops | bytes accessed | tf_op | source)
XLA Modules:
  0.0 82.7 jit_solution(7385257431109838575)
XLA Ops:
  0.6 79.0 %shard_map.76 = (bf16[8,128,1408]{2,1,0:T(8,128)(2,1)S(1)}, bf16[256,1408]{1,0:T(8,128)(2,1)S(1)}, f32[6,128]{1,0:T(8,128)S(1)}) custom-call(bf16[128,2048]{1,0:T(8,128)(2,1)} %tok.1, s32[6,128]{1,0:T(8,128)} %bitcast.12, bf16[6,128]{1,0:T(8,128)(2,1)} %bitcast.13, bf16[8,128,1408]{2,1,0:T(8,128)(2,1)} %bitcast.11, bf16[2048,1408]{1,0:T(8,128)(2,1)} %bitcast.10), custom_call_target="tpu_custom_call" | custom-call | tf_op jit(solution)/shard_map/pallas_call | solution.py:411
  79.6 1.6 %copy.11 = bf16[1,32,32,1408]{3,2,1,0:T(8,128)(2,1)} copy(bf16[1,32,32,1408]{3,2,1,0:T(8,128)(2,1)S(1)} %bitcast.7) | data formatting | bytes 5767168
  81.2 0.9 %copy.12 = bf16[1,256,1408]{2,1,0:T(8,128)(2,1)} copy(bf16[1,256,1408]{2,1,0:T(8,128)(2,1)S(1)} %bitcast.8) | data formatting | bytes 1441792
  82.1 0.6 copy.13
